TPU v7x, 32 devices: a whole 2x2x4 slice. The times are simulated.
32 devices in a mesh: seq: 8 (over z, x), tp: 4 (over y, core).
Axes of the slice: x: 2, y: 2, z: 4, core: 2. Of those that a mesh axis runs over, the one named last changes fastest.
Arguments:
- query_heads: bfloat16 [2048, 2048], P('seq', 'tp'), may hold values from -96 to 96
- key_heads: bfloat16 [2048, 2048], P('seq', 'tp'), may hold values from -4 to 4
- value_heads: bfloat16 [2048, 2048], P('seq', 'tp'), may hold values from -6 to 6
- residual: bfloat16 [2048, 4096], P('seq'), may hold values from -64 to 64
- out_weight: bfloat16 [2048, 4096], P('tp'), may hold values from -0.125 to 0.125
- ln_gain: float32 [4096], replicated, may hold values from 0.1 to 1.9
- up_source: bfloat16 [4096, 4096], P(None, 'tp'), may hold values from -0.09375 to 0.09375
- down_source: bfloat16 [4096, 4096], P('tp'), may hold values from -0.09375 to 0.09375
- copy_gain: float32 [4096], P('tp'), may hold values from 0.3 to 3
- neuron_source: int32 [4096], P('tp'), may hold values from 0 to 4095, as said below
- cotangent: bfloat16 [2048, 4096], P('seq'), may hold values from -6 to 6
Outputs:
- encoded: float32 [2048, 4096], P(('seq', 'tp'))
- grad_query: float32 [2048, 2048], P('seq', 'tp')
- grad_key: float32 [2048, 2048], P('seq', 'tp')
- grad_value: float32 [2048, 2048], P('seq', 'tp')
- grad_residual: float32 [2048, 4096], P('seq', 'tp')
Inputs may be any that keep to these rules, and one draw needn't show every extreme that they name: Added neuron j splits a source neuron of its own group: neuron_source[j] // 1024 == j // 1024.
All inputs are finite; a program needn't handle non-finite values.
Results may differ from a plain program's by a relative error of at most 0.035.
Values may be sent and summed in bfloat16 or wider, within the bound.
A program may use at most 128 MiB of HBM per device.

v0:
```python
import functools
import math

import jax
import jax.numpy as jnp
from jax import lax
from jax.experimental import pallas as pl
from jax.experimental.pallas import tpu as pltpu
from jax.sharding import PartitionSpec as P

HEAD_DIM = 128
OFFSETS = (-2, -1, 1, 2)
CHUNKS = 2
TILE = 512
epsilon = 1e-05
MESH = pl.DeviceIdType.MESH
VM = pltpu.VMEM
F32 = jnp.float32
BF16 = jnp.bfloat16
SCALE = 1.0 / math.sqrt(HEAD_DIM)


def dot_nn(a, b):
    return jnp.dot(a, b, preferred_element_type=F32)


def dot_nt(a, b):
    return lax.dot_general(a, b, (((1,), (1,)), ((), ())), preferred_element_type=F32)


def dot_tn(a, b):
    return lax.dot_general(a, b, (((0,), (0,)), ((), ())), preferred_element_type=F32)


def remote(src, dst, send, recv, **where):
    return pltpu.make_async_remote_copy(
        src_ref=src, dst_ref=dst, send_sem=send, recv_sem=recv, device_id=where, device_id_type=MESH
    )


class Blocks:
    def __init__(self, count):
        self.count = count
        self.place = lax.axis_index("seq")

    def there(self, offset):
        other = self.place + offset
        return (other >= 0) & (other < self.count)

    def greet(self, barrier):
        for offset in OFFSETS:
            @pl.when(self.there(offset))
            def _():
                pl.semaphore_signal(
                    barrier, inc=1, device_id={"seq": self.place + offset}, device_id_type=MESH
                )

    def greeted(self, barrier, more=0):
        peers = sum(self.there(offset).astype(jnp.int32) for offset in OFFSETS)
        pl.semaphore_wait(barrier, peers + more)

    def copy(self, src, window, send, recv, to, slot, sent):
        return remote(src, window.at[slot], send.at[sent], recv.at[slot], seq=self.place + to)

    def send(self, src, window, send, recv):
        for index, offset in enumerate(OFFSETS):
            @pl.when(self.there(offset))
            def _():
                self.copy(src, window, send, recv, offset, 3 - index, index).start()

    def clear(self, window):
        for index, offset in enumerate(OFFSETS):
            @pl.when(jnp.logical_not(self.there(offset)))
            def _():
                window[index] = jnp.zeros(window.shape[1:], window.dtype)

    def arrive(self, src, window, send, recv, index):
        offset = OFFSETS[index]
        @pl.when(self.there(offset))
        def _():
            self.copy(src, window, send, recv, offset, index, index).wait_recv()

    def left(self, src, window, send, recv):
        for index, offset in enumerate(OFFSETS):
            @pl.when(self.there(offset))
            def _():
                self.copy(src, window, send, recv, offset, 3 - index, index).wait_send()


class Group:
    def __init__(self):
        me = lax.axis_index("tp")
        chip, core = lax.div(me, 2), lax.rem(me, 2)
        self.me = me
        self.sibling = chip * 2 + 1 - core
        self.far = (1 - chip) * 2 + core
        self.across = (1 - chip) * 2 + 1 - core

    def greet(self, barrier):
        for other in (self.sibling, self.far):
            pl.semaphore_signal(barrier, inc=1, device_id={"tp": other}, device_id_type=MESH)


def attend_kernel(
    count, q_ref, k_ref, v_ref, out_ref, kwin, vwin, stat_ref, prob, ks, kr, vs, vr
):
    blocks = Blocks(count)
    barrier = pltpu.get_barrier_semaphore()
    blocks.greet(barrier)
    blocks.greeted(barrier)
    blocks.send(k_ref, kwin, ks, kr)
    blocks.send(v_ref, vwin, vs, vr)
    blocks.clear(kwin)
    blocks.clear(vwin)
    rows, width = q_ref.shape
    heads = width // HEAD_DIM
    for index in range(4):
        blocks.arrive(k_ref, kwin, ks, kr, index)
    bias = [jnp.where(blocks.there(offset), 0.0, -1e30).astype(F32) for offset in OFFSETS]
    lane = lax.broadcasted_iota(jnp.int32, (rows, 128), 1)
    stats = jnp.zeros((rows, 128), F32)
    for h in range(heads):
        cols = slice(h * HEAD_DIM, (h + 1) * HEAD_DIM)
        qh = q_ref[:, cols]
        scores = [dot_nt(qh, k_ref[:, cols]) * SCALE]
        for index in range(4):
            scores.append(dot_nt(qh, kwin[index, :, cols]) * SCALE + bias[index])
        top = scores[0]
        for s in scores[1:]:
            top = jnp.maximum(top, s)
        top = jnp.max(top, axis=1, keepdims=True)
        exps = [jnp.exp(s - top) for s in scores]
        total = exps[0]
        for e in exps[1:]:
            total = total + e
        inverse = 1.0 / jnp.sum(total, axis=1, keepdims=True)
        for index in range(5):
            prob[h, index] = (exps[index] * inverse).astype(BF16)
        stats = jnp.where(lane == h, top, stats)
        stats = jnp.where(lane == heads + h, inverse, stats)
    stat_ref[...] = jnp.transpose(stats)[: 2 * heads]
    for index in range(4):
        blocks.arrive(v_ref, vwin, vs, vr, index)
    for h in range(heads):
        cols = slice(h * HEAD_DIM, (h + 1) * HEAD_DIM)
        acc = dot_nn(prob[h, 0], v_ref[:, cols])
        for index in range(4):
            acc = acc + dot_nn(prob[h, index + 1], vwin[index, :, cols])
        out_ref[:, cols] = acc.astype(BF16)
    blocks.left(k_ref, kwin, ks, kr)
    blocks.left(v_ref, vwin, vs, vr)


def attend(count, q, k, v):
    rows, width = q.shape
    heads = width // HEAD_DIM
    win = jax.ShapeDtypeStruct((4, rows, width), BF16)
    dma = pltpu.SemaphoreType.DMA((4,))
    return pl.pallas_call(
        functools.partial(attend_kernel, count),
        out_shape=(
            jax.ShapeDtypeStruct((rows, width), BF16),
            win,
            win,
            jax.ShapeDtypeStruct((2 * heads, rows), F32),
        ),
        in_specs=[pl.BlockSpec(memory_space=VM)] * 3,
        out_specs=(pl.BlockSpec(memory_space=VM),) * 4,
        scratch_shapes=[VM((heads, 5, rows, rows), BF16), dma, dma, dma, dma],
        compiler_params=pltpu.CompilerParams(
            collective_id=1, has_side_effects=True, vmem_limit_bytes=32 << 20
        ),
        name="attend",
    )(q, k, v)


def reduce_first(group, own, part, mine, sbuf1, rbuf1, s1, r1):
    part((group.across, group.sibling), sbuf1)
    copies = [
        remote(sbuf1.at[i], rbuf1.at[i], s1.at[i], r1.at[i], tp=group.sibling) for i in range(2)
    ]
    for copy in copies:
        copy.start()
    part((group.far, group.me), mine)
    return copies


def reduce_second(group, own, mine, rbuf1, sbuf2, rbuf2, s2, r2, copies):
    copies[0].wait_recv()
    rows = own // CHUNKS
    out = []
    for ch in range(CHUNKS):
        sl = slice(ch * rows, (ch + 1) * rows)
        sbuf2[ch] = (mine[0, sl].astype(F32) + rbuf1[0, sl].astype(F32)).astype(BF16)
        copy = remote(sbuf2.at[ch], rbuf2.at[ch], s2.at[ch], r2.at[ch], tp=group.far)
        copy.start()
        out.append(copy)
    copies[1].wait_recv()
    return out


def spread(group, own, full, finish, seconds, ags, agr):
    rows = own // CHUNKS

    def at(owner, ch):
        return full.at[pl.ds(pl.multiple_of(owner * own + ch * rows, rows), rows)]

    to_sib, to_far, passed = [], [], []
    for ch in range(CHUNKS):
        seconds[ch].wait_recv()
        finish(ch, at(group.me, ch))
        mine = at(group.me, ch)
        to_far.append(remote(mine, mine, ags.at[ch, 0], agr.at[ch, 0], tp=group.far))
        to_far[ch].start()
        to_sib.append(remote(mine, mine, ags.at[ch, 1], agr.at[ch, 1], tp=group.sibling))
        to_sib[ch].start()
    for ch in range(CHUNKS):
        to_far[ch].wait_recv()
        got = at(group.far, ch)
        passed.append(remote(got, got, ags.at[ch, 2], agr.at[ch, 2], tp=group.sibling))
        passed[ch].start()
    for ch in range(CHUNKS):
        to_sib[ch].wait_recv()
        passed[ch].wait_recv()
    return to_sib + to_far + passed


def norm_kernel(
    count, att_ref, w_ref, res_ref, gain_ref, q_ref, stat_ref,
    full, unit_ref, sigma_ref, qwin, swin,
    mine, sbuf1, rbuf1, sbuf2, rbuf2, res_buf,
    s1, r1, s2, r2, ags, agr, qs, qr, ss, sr, res_sem,
):
    blocks, group = Blocks(count), Group()
    own, width = unit_ref.shape
    rows = own // CHUNKS
    fetch = pltpu.make_async_copy(
        res_ref.at[pl.ds(pl.multiple_of(group.me * own, own), own)], res_buf, res_sem
    )
    fetch.start()
    barrier = pltpu.get_barrier_semaphore()
    group.greet(barrier)
    blocks.greet(barrier)
    blocks.greeted(barrier, 2)
    blocks.send(q_ref, qwin, qs, qr)
    blocks.send(stat_ref, swin, ss, sr)

    def part(owners, dst):
        lhs = jnp.concatenate(
            [att_ref[pl.ds(pl.multiple_of(o * own, own), own), :] for o in owners], axis=0
        )

        @pl.loop(0, width // TILE)
        def _(ct):
            cols = pl.ds(pl.multiple_of(ct * TILE, TILE), TILE)
            r = dot_nn(lhs, w_ref[:, cols]).astype(BF16)
            dst[0, :, cols] = r[:own]
            dst[1, :, cols] = r[own:]

    firsts = reduce_first(group, own, part, mine, sbuf1, rbuf1, s1, r1)
    blocks.clear(qwin)
    blocks.clear(swin)
    seconds = reduce_second(group, own, mine, rbuf1, sbuf2, rbuf2, s2, r2, firsts)
    fetch.wait()

    def finish(ch, dst):
        sl = slice(ch * rows, (ch + 1) * rows)
        stream = (
            res_buf[sl].astype(F32)
            + mine[1, sl].astype(F32)
            + rbuf1[1, sl].astype(F32)
            + rbuf2[ch].astype(F32)
        )
        centered = stream - jnp.mean(stream, axis=1, keepdims=True)
        sigma = jnp.sqrt(jnp.mean(centered * centered, axis=1, keepdims=True) + epsilon)
        unit = centered / sigma
        unit_ref[sl] = unit
        sigma_ref[sl] = jnp.broadcast_to(sigma, (rows, 128))
        dst[...] = (unit * gain_ref[...]).astype(BF16)

    tails = spread(group, own, full, finish, seconds, ags, agr)
    for copy in firsts + seconds + tails:
        copy.wait_send()
    for index in range(4):
        blocks.arrive(q_ref, qwin, qs, qr, index)
        blocks.arrive(stat_ref, swin, ss, sr, index)
    blocks.left(q_ref, qwin, qs, qr)
    blocks.left(stat_ref, swin, ss, sr)


def reduce_scratch(own, width):
    two = VM((2, own, width), BF16)
    chunk = VM((CHUNKS, own // CHUNKS, width), BF16)
    return [two, two, two, chunk, chunk]


def reduce_sems():
    dma = pltpu.SemaphoreType.DMA
    return [dma((2,)), dma((2,)), dma((CHUNKS,)), dma((CHUNKS,))]


def norm_stage(count, groups, att, w, residual, gain, q, stats):
    tok, width = residual.shape
    own = tok // groups
    dma = pltpu.SemaphoreType.DMA
    vm = pl.BlockSpec(memory_space=VM)
    return pl.pallas_call(
        functools.partial(norm_kernel, count),
        out_shape=(
            jax.ShapeDtypeStruct((tok, width), BF16),
            jax.ShapeDtypeStruct((own, width), F32),
            jax.ShapeDtypeStruct((own, 128), F32),
            jax.ShapeDtypeStruct((4,) + q.shape, BF16),
            jax.ShapeDtypeStruct((4,) + stats.shape, F32),
        ),
        in_specs=[vm, vm, pl.BlockSpec(memory_space=pl.ANY), vm, vm, vm],
        out_specs=(vm,) * 5,
        scratch_shapes=reduce_scratch(own, width)
        + [VM((own, width), BF16)]
        + reduce_sems()
        + [dma((CHUNKS, 3)), dma((CHUNKS, 3))]
        + [dma((4,))] * 4
        + [dma(())],
        compiler_params=pltpu.CompilerParams(
            collective_id=2, has_side_effects=True, vmem_limit_bytes=40 << 20
        ),
        name="norm_stage",
    )(att, w, residual, gain, q, stats)


def back_kernel(
    gh_ref, w_ref, cot_ref, gain_ref, unit_ref, sigma_ref,
    full,
    mine, sbuf1, rbuf1, sbuf2, rbuf2, cot_buf,
    s1, r1, s2, r2, ags, agr, cot_sem,
):
    group = Group()
    own, width = unit_ref.shape
    rows = own // CHUNKS
    fetch = pltpu.make_async_copy(
        cot_ref.at[pl.ds(pl.multiple_of(group.me * own, own), own)], cot_buf, cot_sem
    )
    fetch.start()
    barrier = pltpu.get_barrier_semaphore()
    group.greet(barrier)
    pl.semaphore_wait(barrier, 2)

    def part(owners, dst):
        lhs = jnp.concatenate(
            [gh_ref[pl.ds(pl.multiple_of(o * own, own), own), :] for o in owners], axis=0
        )

        @pl.loop(0, width // TILE)
        def _(ct):
            cols = pl.ds(pl.multiple_of(ct * TILE, TILE), TILE)
            r = dot_nt(lhs, w_ref[cols, :]).astype(BF16)
            dst[0, :, cols] = r[:own]
            dst[1, :, cols] = r[own:]

    firsts = reduce_first(group, own, part, mine, sbuf1, rbuf1, s1, r1)
    seconds = reduce_second(group, own, mine, rbuf1, sbuf2, rbuf2, s2, r2, firsts)
    fetch.wait()

    def finish(ch, dst):
        sl = slice(ch * rows, (ch + 1) * rows)
        grad = (
            cot_buf[sl].astype(F32)
            + mine[1, sl].astype(F32)
            + rbuf1[1, sl].astype(F32)
            + rbuf2[ch].astype(F32)
        )
        scaled = grad * gain_ref[...]
        unit = unit_ref[sl]
        mean = jnp.mean(scaled, axis=1, keepdims=True)
        along = jnp.mean(scaled * unit, axis=1, keepdims=True)
        dst[...] = ((scaled - mean - unit * along) / sigma_ref[sl, :1]).astype(BF16)

    tails = spread(group, own, full, finish, seconds, ags, agr)
    for copy in firsts + seconds + tails:
        copy.wait_send()


def back_stage(groups, gh, w, cotangent, gain, unit, sigma):
    tok, width = cotangent.shape
    own = tok // groups
    dma = pltpu.SemaphoreType.DMA
    vm = pl.BlockSpec(memory_space=VM)
    return pl.pallas_call(
        back_kernel,
        out_shape=jax.ShapeDtypeStruct((tok, width), BF16),
        in_specs=[vm, vm, pl.BlockSpec(memory_space=pl.ANY), vm, vm, vm],
        out_specs=vm,
        scratch_shapes=reduce_scratch(own, width)
        + [VM((own, width), BF16)]
        + reduce_sems()
        + [dma((CHUNKS, 3)), dma((CHUNKS, 3)), dma(())],
        compiler_params=pltpu.CompilerParams(
            collective_id=3, has_side_effects=True, vmem_limit_bytes=40 << 20
        ),
        name="back_stage",
    )(gh, w, cotangent, gain, unit, sigma)


def grads_kernel(
    count, low_ref, w_ref, att_ref, q_ref, k_ref, v_ref, kwin, vwin, qwin, stat_ref, swin,
    ffn_ref, unit_ref, gain_ref,
    enc_ref, gq_ref, gk_ref, gv_ref,
    dwin, twin, do_ref, delta_ref, rbuf1, sbuf2, rbuf2,
    ds_, dr, ts, tr, s1, r1, s2, r2,
):
    blocks, group = Blocks(count), Group()
    own, width = unit_ref.shape
    tok, cols_all = q_ref.shape
    heads = cols_all // HEAD_DIM
    rows = own // CHUNKS
    barrier = pltpu.get_barrier_semaphore()
    group.greet(barrier)
    blocks.greet(barrier)
    blocks.greeted(barrier, 2)

    def ffn_rows(owner):
        return ffn_ref.at[pl.ds(pl.multiple_of(owner * own, own), own)]

    firsts = [
        remote(ffn_rows(owner), rbuf1.at[i], s1.at[i], r1.at[i], tp=group.sibling)
        for i, owner in enumerate((group.across, group.sibling))
    ]
    for copy in firsts:
        copy.start()
    lane = lax.broadcasted_iota(jnp.int32, (tok, 128), 1)
    grad_att = dot_nt(low_ref[...], w_ref[...]).astype(BF16)
    do_ref[...] = grad_att
    blocks.send(do_ref, dwin, ds_, dr)
    deltas = jnp.zeros((tok, 128), F32)
    for h in range(heads):
        cols = slice(h * HEAD_DIM, (h + 1) * HEAD_DIM)
        delta = jnp.sum(
            grad_att[:, cols].astype(F32) * att_ref[:, cols].astype(F32), axis=1, keepdims=True
        )
        deltas = jnp.where(lane == h, delta, deltas)
    delta_ref[...] = jnp.transpose(deltas)[:8]
    blocks.send(delta_ref, twin, ts, tr)
    blocks.clear(dwin)
    blocks.clear(twin)
    firsts[0].wait_recv()
    seconds = []
    far_rows = ffn_rows(group.far)
    for ch in range(CHUNKS):
        sl = slice(ch * rows, (ch + 1) * rows)
        sbuf2[ch] = (far_rows[sl].astype(F32) + rbuf1[0, sl].astype(F32)).astype(BF16)
        seconds.append(remote(sbuf2.at[ch], rbuf2.at[ch], s2.at[ch], r2.at[ch], tp=group.far))
        seconds[ch].start()

    def pair(queries, keys, values, grads, stats, delta_row, h):
        top = stats[pl.ds(h, 1), :]
        inverse = stats[pl.ds(heads + h, 1), :]
        prob = jnp.exp(dot_nt(keys, queries) * SCALE - top) * inverse
        slope = (prob * (dot_nt(values, grads) - delta_row[pl.ds(h, 1), :])).astype(BF16)
        return prob.astype(BF16), slope

    @pl.loop(0, heads)
    def _(h):
        cols = pl.ds(pl.multiple_of(h * HEAD_DIM, HEAD_DIM), HEAD_DIM)
        qh, gh = q_ref[:, cols], do_ref[:, cols]
        kh, vh = k_ref[:, cols], v_ref[:, cols]
        prob, slope = pair(qh, kh, vh, gh, stat_ref, delta_ref, h)
        gv_ref[:, cols] = dot_nn(prob, gh)
        gk_ref[:, cols] = dot_nn(slope, qh)
        acc = dot_tn(slope, kh)
        for index in range(4):
            k_off, v_off = kwin[index, :, cols], vwin[index, :, cols]
            live = jnp.where(blocks.there(OFFSETS[index]), 1.0, 0.0).astype(F32)
            _, slope = pair_off(qh, k_off, v_off, gh, stat_ref, delta_ref, h, live)
            acc = acc + dot_tn(slope, k_off)
        gq_ref[:, cols] = acc * SCALE

    for index in range(4):
        blocks.arrive(do_ref, dwin, ds_, dr, index)
        blocks.arrive(delta_ref, twin, ts, tr, index)

    @pl.loop(0, heads)
    def _(h):
        cols = pl.ds(pl.multiple_of(h * HEAD_DIM, HEAD_DIM), HEAD_DIM)
        kh, vh = k_ref[:, cols], v_ref[:, cols]
        gv, gk = gv_ref[:, cols], gk_ref[:, cols]
        for index in range(4):
            q_off, g_off = qwin[index, :, cols], dwin[index, :, cols]
            prob, slope = pair(q_off, kh, vh, g_off, swin.at[index], twin.at[index], h)
            gv = gv + dot_nn(prob, g_off)
            gk = gk + dot_nn(slope, q_off)
        gv_ref[:, cols] = gv
        gk_ref[:, cols] = gk * SCALE

    firsts[1].wait_recv()
    near_rows = ffn_rows(group.me)
    for ch in range(CHUNKS):
        sl = slice(ch * rows, (ch + 1) * rows)
        seconds[ch].wait_recv()
        enc_ref[sl] = unit_ref[sl] * gain_ref[...] + (
            near_rows[sl].astype(F32) + rbuf1[1, sl].astype(F32) + rbuf2[ch].astype(F32)
        )
    for copy in firsts + seconds:
        copy.wait_send()
    blocks.left(do_ref, dwin, ds_, dr)
    blocks.left(delta_ref, twin, ts, tr)


def pair_off(queries, keys, values, grads, stats, delta_row, h, live):
    heads = stats.shape[0] // 2
    bias = (live - 1.0) * 1e30
    prob = jnp.exp(dot_nt(keys, queries) * SCALE + bias - stats[pl.ds(h, 1), :])
    prob = prob * stats[pl.ds(heads + h, 1), :]
    slope = (prob * (dot_nt(values, grads) - delta_row[pl.ds(h, 1), :])).astype(BF16)
    return None, slope


def grads_stage(count, low, w, att, q, k, v, kwin, vwin, qwin, stats, swin, ffn, unit, gain):
    tok, width = low.shape
    own = unit.shape[0]
    dma = pltpu.SemaphoreType.DMA
    vm = pl.BlockSpec(memory_space=VM)
    chunk = VM((CHUNKS, own // CHUNKS, width), BF16)
    grad = jax.ShapeDtypeStruct(q.shape, F32)
    return pl.pallas_call(
        functools.partial(grads_kernel, count),
        out_shape=(jax.ShapeDtypeStruct((own, width), F32), grad, grad, grad),
        in_specs=[vm] * 14,
        out_specs=(vm,) * 4,
        scratch_shapes=[
            VM((4,) + q.shape, BF16),
            VM((4, 8, tok), F32),
            VM(q.shape, BF16),
            VM((8, tok), F32),
            VM((2, own, width), BF16),
            chunk,
            chunk,
        ]
        + [dma((4,))] * 4
        + reduce_sems(),
        compiler_params=pltpu.CompilerParams(
            collective_id=4, has_side_effects=True, vmem_limit_bytes=48 << 20
        ),
        name="grads_stage",
    )(low, w, att, q, k, v, kwin, vwin, qwin, stats, swin, ffn, unit, gain)


def gelu_slope(inputs):
    output, pull_back = jax.vjp(jax.nn.gelu, inputs)
    return (output, pull_back(jnp.ones_like(inputs))[0])


def shards(
    count,
    groups,
    query_heads,
    key_heads,
    value_heads,
    residual,
    out_weight,
    ln_gain,
    up_source,
    down_source,
    copy_gain,
    neuron_source,
    cotangent,
):
    model_width = residual.shape[1]
    tp_place = lax.axis_index("tp")
    gain = ln_gain[None, :]
    src_width = up_source.shape[1]
    local_source = neuron_source - tp_place * src_width
    pick = (
        lax.broadcasted_iota(jnp.int32, (src_width, local_source.shape[0]), 0)
        == local_source[None, :]
    )
    counts = 1.0 + jnp.sum(pick.astype(F32), axis=1)
    inverse = 1.0 / counts
    pick = pick.astype(BF16)

    attended, kwin, vwin, stats = attend(count, query_heads, key_heads, value_heads)
    normed, unit, sigma, qwin, swin = norm_stage(
        count, groups, attended, out_weight, residual, gain, query_heads, stats
    )
    hidden_in = dot_nn(normed, up_source)
    copies_in = dot_nn(hidden_in.astype(BF16), pick) * copy_gain
    act_src, slope_src = gelu_slope(hidden_in)
    act_copy, slope_copy = gelu_slope(copies_in)
    merged = ((act_src + dot_nt(act_copy.astype(BF16), pick)) * inverse).astype(BF16)
    grad_scaled = dot_nt(cotangent, down_source) * inverse
    grad_copy = dot_nn(grad_scaled.astype(BF16), pick) * slope_copy
    grad_hidden = (
        grad_scaled * slope_src + dot_nt((grad_copy * copy_gain).astype(BF16), pick)
    ).astype(BF16)
    ffn_part = dot_nn(merged, down_source).astype(BF16)
    grad_low = back_stage(groups, grad_hidden, up_source, cotangent, gain, unit, sigma)
    encoded, grad_query, grad_key, grad_value = grads_stage(
        count, grad_low, out_weight, attended, query_heads, key_heads, value_heads,
        kwin, vwin, qwin, stats, swin, ffn_part, unit, gain,
    )
    col_width = model_width // groups
    grad_residual = lax.dynamic_slice_in_dim(grad_low, tp_place * col_width, col_width, 1)
    return (encoded, grad_query, grad_key, grad_value, grad_residual.astype(F32))


def solution(mesh):
    in_specs = (
        P("seq", "tp"),
        P("seq", "tp"),
        P("seq", "tp"),
        P("seq", None),
        P("tp", None),
        P(),
        P(None, "tp"),
        P("tp", None),
        P("tp"),
        P("tp"),
        P("seq", None),
    )
    out_specs = (
        P(("seq", "tp"), None),
        P("seq", "tp"),
        P("seq", "tp"),
        P("seq", "tp"),
        P("seq", "tp"),
    )
    body = functools.partial(shards, mesh.shape["seq"], mesh.shape["tp"])
    return jax.shard_map(body, mesh=mesh, in_specs=in_specs, out_specs=out_specs, check_vma=False)
```

profile of v0, /device:TPU:10, one launch (start us, length us, event | category | flops | bytes accessed | tf_op | source)
XLA Modules:
  0.0 162.0 jit_solution(9899816991149960115)
XLA Ops:
  0.6 0.7 broadcast_subtract_fusion
  1.3 0.5 convert_reduce_fusion
  1.8 0.0 slice-start
  1.8 0.0 copy-start.4
  1.9 0.0 copy-start.12
  1.9 0.0 copy-start
  1.9 0.0 copy-start.5
  1.9 0.0 copy-start.19
  1.9 0.0 slice-start.1
  1.9 7.5 %convolution_multiply_fusion = f32[256,1024]{1,0:T(8,128)} fusion(bf16[256,4096]{1,0:T(8,128)(2,1)} %cot_ref.1, bf16[1024,4096]{1,0:T(8,128)(2,1)} %param.18, f32[1024]{0:T(1024)S(1)} %add_divide_fusion), kind=kOutput, calls=%fused_computation.21 | convolution fusion | flops 2147745792 | bytes 11538432 | tf_op jit(solution)/shard_map/dot_general | solution.py:28
  9.4 0.0 copy-done.4
  9.4 0.0 copy-done.12
  9.4 0.0 copy-start.14
  9.4 1.2 copy-done.14
  10.7 27.0 %attend.1 = (bf16[256,512]{1,0:T(8,128)(2,1)S(1)}, bf16[4,256,512]{2,1,0:T(8,128)(2,1)S(1)}, bf16[4,256,512]{2,1,0:T(8,128)(2,1)S(1)}, f32[8,256]{1,0:T(8,128)S(1)}) custom-call(bf16[256,512]{1,0:T(8,128)(2,1)S(1)} %copy-done.4, bf16[256,512]{1,0:T(8,128)(2,1)S(1)} %copy-done.12, bf16[256,512]{1,0:T(8,128)(2,1)S(1)} %copy-done.14), custom_call_target="tpu_custom_call" | custom-call | tf_op jit(solution)/shard_map/attend/pallas_call | solution.py:159
  37.7 0.0 copy-start.7
  37.7 1.0 copy-done.7
  38.7 1.0 copy-done.9
  39.7 0.0 copy-start.16
  39.7 0.0 copy-done
  39.7 0.0 copy-done.5
  39.7 0.0 copy-done.19
  39.7 31.8 %norm_stage.1 = (bf16[256,4096]{1,0:T(8,128)(2,1)S(1)}, f32[64,4096]{1,0:T(8,128)S(1)}, f32[64,128]{1,0:T(8,128)S(1)}, bf16[4,256,512]{2,1,0:T(8,128)(2,1)S(1)}, f32[4,8,256]{2,1,0:T(8,128)S(1)}) custom-call(bf16[256,512]{1,0:T(8,128)(2,1)S(1)} %get-tuple-element.18.att_ref, bf16[512,4096]{1,0:T(8,128)(2,1)S(1)} %copy-done, bf16[256,4096]{1,0:T(8,128)(2,1)S(1)} %copy-done.5, ...), custom_call_target="tpu_custom_call" | custom-call | tf_op jit(solution)/shard_map/norm_stage/pallas_call | solution.py:307
  71.5 0.0 copy-start.11
  71.5 0.0 copy-start.3
  71.5 0.0 slice-done
  71.5 0.0 slice-done.1
  71.6 0.0 copy-start.20
  71.6 2.3 %fusion.67 = f32[256,1024]{1,0:T(8,128)S(1)} fusion(bf16[256,4096]{1,0:T(8,128)(2,1)S(1)} %get-tuple-element.20, bf16[4096,1024]{1,0:T(8,128)(2,1)S(1)} %bitcast.7), kind=kOutput, calls=%fused_computation.68 | convolution fusion | flops 2147483648 | bytes 11534336 | tf_op jit(solution)/shard_map/dot_general | solution.py:24
  73.9 0.0 copy-done.16
  73.9 0.0 copy-done.11
  73.9 0.0 copy-done.20
  73.9 0.0 copy-start.21
  73.9 1.0 fusion.10
  74.9 0.0 copy-done.21
  75.0 0.0 copy-start.22
  75.0 0.9 copy-done.22
  75.9 5.5 %fusion.15.gh_ref = bf16[256,1024]{1,0:T(8,128)(2,1)} fusion(s32[1024]{0:T(1024)S(1)} %broadcast_subtract_fusion, f32[256,1024]{1,0:T(8,128)} %convolution_multiply_fusion, f32[256,1024]{1,0:T(8,128)S(1)} %fusion.67, f32[256,1024]{1,0:T(8,128)S(1)} %fusion.10, f32[1024]{0:T(1024)S(1)} %copy-done.20), kind=kOutput, calls=%fused_computation.23 | convolution fusion | flops 1086586880 | bytes 3678208 | tf_op jit(solution)/shard_map/dot_general | solution.py:28
  81.4 0.0 copy-start.6
  81.4 9.2 %convolution_convert_fusion.ffn_ref = bf16[256,4096]{1,0:T(8,128)(2,1)} fusion(bf16[1024,4096]{1,0:T(8,128)(2,1)} %param.18, s32[1024]{0:T(1024)S(1)} %broadcast_subtract_fusion, f32[256,1024]{1,0:T(8,128)} %copy-done.21, f32[256,1024]{1,0:T(8,128)} %copy-done.22, f32[1024]{0:T(1024)S(1)} %add_divide_fusion), kind=kOutput, calls=%fused_computation | convolution fusion | flops 2691694592 | bytes 12591104 | tf_op jit(solution)/shard_map/dot_general | solution.py:24
  90.6 0.0 copy-done.3
  90.6 0.0 copy-done.6
  90.6 0.0 copy-start.2
  90.6 3.4 %copy-done.2 = bf16[4096,1024]{1,0:T(8,128)(2,1)S(1)} copy-done((bf16[4096,1024]{1,0:T(8,128)(2,1)S(1)}, bf16[4096,1024]{1,0:T(8,128)(2,1)}, u32[]{:S(2)}) %copy-start.2) | copy-done | bytes 8388632
  94.0 0.0 copy-start.18
  94.0 1.0 copy-done.18
  95.1 0.0 copy-start.8
  95.1 0.0 copy-start.10
  95.1 0.0 copy-start.13
  95.1 0.0 copy-start.17
  95.1 34.7 %back_stage.1.low_ref = bf16[256,4096]{1,0:T(8,128)(2,1)S(1)} custom-call(bf16[256,1024]{1,0:T(8,128)(2,1)S(1)} %copy-done.18, bf16[4096,1024]{1,0:T(8,128)(2,1)S(1)} %copy-done.2, bf16[256,4096]{1,0:T(8,128)(2,1)S(1)} %copy-done.6, f32[1,4096]{1,0:T(1,128)S(1)} %bitcast.9, f32[64,4096]{1,0:T(8,128)S(1)} %get-tuple-element.21.unit_ref, ...), custom_call_target="tpu_custom_call" | custom-call | tf_op jit(solution)/shard_map/back_stage/pallas_call | solution.py:388
  129.8 0.0 copy-start.1
  129.8 1.3 copy-done.1
  131.1 0.0 copy-done.8
  131.1 0.0 copy-done.10
  131.1 0.0 copy-done.13
  131.1 0.0 copy-done.15
  131.1 0.0 copy-done.17
  131.1 25.4 %grads_stage.1 = (f32[64,4096]{1,0:T(8,128)S(1)}, f32[256,512]{1,0:T(8,128)S(1)}, f32[256,512]{1,0:T(8,128)S(1)}, f32[256,512]{1,0:T(8,128)S(1)}) custom-call(bf16[256,4096]{1,0:T(8,128)(2,1)} %copy-done.1, bf16[512,4096]{1,0:T(8,128)(2,1)} %w_ref.5, bf16[256,512]{1,0:T(8,128)(2,1)S(1)} %copy-done.17, bf16[256,512]{1,0:T(8,128)(2,1)S(1)} %copy-done.4, ...), custom_call_target="tpu_custom_call" | custom-call | tf_op jit(solution)/shard_map/grads_stage/pallas_call | solution.py:524
  156.5 2.1 %dynamic-slice_convert_fusion = f32[256,1024]{1,0:T(8,128)} fusion(bf16[256,4096]{1,0:T(8,128)(2,1)} %copy-done.1, s32[]{:T(128)S(6)} %select_n.3), kind=kLoop, calls=%fused_computation.41 | loop fusion | flops 262144 | bytes 1572868 | tf_op jit(solution)/shard_map/convert_element_type | solution.py:602
  158.7 1.0 copy.20
  159.6 0.8 copy.21
  160.4 0.8 copy.22
  161.2 0.8 copy.23
  (4 shorter events, 0.0 us)
Async XLA Ops:
  1.8 69.7 %slice-start = ((s8[8388608]{0:T(1024)(128)(4,1)}), s8[4194304]{0:T(1024)(128)(4,1)S(1)}, s32[]{:S(2)}) async-start(s8[8388608]{0:T(1024)(128)(4,1)} %bitcast.6), calls=%async_computation | async-start | bytes 8388608
  1.8 7.6 %copy-start.4 = (bf16[256,512]{1,0:T(8,128)(2,1)S(1)}, bf16[256,512]{1,0:T(8,128)(2,1)}, u32[]{:S(2)}) copy-start(bf16[256,512]{1,0:T(8,128)(2,1)} %q_ref.5) | copy-start | bytes 786436
  1.9 7.6 %copy-start.12 = (bf16[256,512]{1,0:T(8,128)(2,1)S(1)}, bf16[256,512]{1,0:T(8,128)(2,1)}, u32[]{:S(2)}) copy-start(bf16[256,512]{1,0:T(8,128)(2,1)} %k_ref.3) | copy-start | bytes 786436
  1.9 37.8 %copy-start = (bf16[512,4096]{1,0:T(8,128)(2,1)S(1)}, bf16[512,4096]{1,0:T(8,128)(2,1)}, u32[]{:S(2)}) copy-start(bf16[512,4096]{1,0:T(8,128)(2,1)} %w_ref.5) | copy-start | bytes 12582916
  1.9 37.8 %copy-start.5 = (bf16[256,4096]{1,0:T(8,128)(2,1)S(1)}, bf16[256,4096]{1,0:T(8,128)(2,1)}, u32[]{:S(2)}) copy-start(bf16[256,4096]{1,0:T(8,128)(2,1)} %res_ref.1) | copy-start | bytes 6291460
  1.9 37.8 %copy-start.19 = (f32[4096]{0:T(1024)S(1)}, f32[4096]{0:T(1024)}, u32[]{:S(2)}) copy-start(f32[4096]{0:T(1024)} %param.16) | copy-start | bytes 49156
  1.9 69.6 %slice-start.1 = ((s8[8388608]{0:T(1024)(128)(4,1)}), s8[4194304]{0:T(1024)(128)(4,1)S(1)}, s32[]{:S(2)}) async-start(s8[8388608]{0:T(1024)(128)(4,1)} %bitcast.6), calls=%async_computation.1 | async-start | bytes 8388608
  9.4 1.2 copy-start.14
  37.7 1.0 copy-start.7
  38.7 1.0 copy-start.9
  39.7 34.2 %copy-start.16 = (bf16[256,512]{1,0:T(8,128)(2,1)}, bf16[256,512]{1,0:T(8,128)(2,1)S(1)}, u32[]{:S(2)}) copy-start(bf16[256,512]{1,0:T(8,128)(2,1)S(1)} %get-tuple-element.18.att_ref) | copy-start | bytes 786436
  71.5 2.4 %copy-start.11 = (bf16[4,256,512]{2,1,0:T(8,128)(2,1)}, bf16[4,256,512]{2,1,0:T(8,128)(2,1)S(1)}, u32[]{:S(2)}) copy-start(bf16[4,256,512]{2,1,0:T(8,128)(2,1)S(1)} %get-tuple-element.25.qwin) | copy-start | bytes 3145732
  71.5 19.1 %copy-start.3 = (f32[64,4096]{1,0:T(8,128)}, f32[64,4096]{1,0:T(8,128)S(1)}, u32[]{:S(2)}) copy-start(f32[64,4096]{1,0:T(8,128)S(1)} %get-tuple-element.21.unit_ref) | copy-start | bytes 3145732
  71.6 2.4 %copy-start.20 = (f32[1024]{0:T(1024)S(1)}, f32[1024]{0:T(1024)}, u32[]{:S(2)}) copy-start(f32[1024]{0:T(1024)} %param.19) | copy-start | bytes 12292
  73.9 1.0 copy-start.21
  75.0 1.0 copy-start.22
  81.4 9.2 %copy-start.6 = (bf16[256,4096]{1,0:T(8,128)(2,1)S(1)}, bf16[256,4096]{1,0:T(8,128)(2,1)}, u32[]{:S(2)}) copy-start(bf16[256,4096]{1,0:T(8,128)(2,1)} %cot_ref.1) | copy-start | bytes 6291460
  90.6 3.4 %copy-start.2 = (bf16[4096,1024]{1,0:T(8,128)(2,1)S(1)}, bf16[4096,1024]{1,0:T(8,128)(2,1)}, u32[]{:S(2)}) copy-start(bf16[4096,1024]{1,0:T(8,128)(2,1)} %w_ref.4) | copy-start | bytes 25165828
  94.0 1.0 copy-start.18
  95.1 36.0 %copy-start.8 = (bf16[4,256,512]{2,1,0:T(8,128)(2,1)S(1)}, bf16[4,256,512]{2,1,0:T(8,128)(2,1)}, u32[]{:S(2)}) copy-start(bf16[4,256,512]{2,1,0:T(8,128)(2,1)} %copy-done.7) | copy-start | bytes 3145732
  95.1 36.0 %copy-start.10 = (bf16[4,256,512]{2,1,0:T(8,128)(2,1)S(1)}, bf16[4,256,512]{2,1,0:T(8,128)(2,1)}, u32[]{:S(2)}) copy-start(bf16[4,256,512]{2,1,0:T(8,128)(2,1)} %copy-done.9) | copy-start | bytes 3145732
  95.1 36.0 %copy-start.13 = (bf16[256,512]{1,0:T(8,128)(2,1)S(1)}, bf16[256,512]{1,0:T(8,128)(2,1)}, u32[]{:S(2)}) copy-start(bf16[256,512]{1,0:T(8,128)(2,1)} %k_ref.3) | copy-start | bytes 786436
  95.1 36.0 %copy-start.15 = (bf16[256,512]{1,0:T(8,128)(2,1)S(1)}, bf16[256,512]{1,0:T(8,128)(2,1)}, u32[]{:S(2)}) copy-start(bf16[256,512]{1,0:T(8,128)(2,1)} %v_ref.3) | copy-start | bytes 786436
  95.1 36.0 %copy-start.17 = (bf16[256,512]{1,0:T(8,128)(2,1)S(1)}, bf16[256,512]{1,0:T(8,128)(2,1)}, u32[]{:S(2)}) copy-start(bf16[256,512]{1,0:T(8,128)(2,1)} %copy-done.16) | copy-start | bytes 786436
  129.8 1.3 copy-start.1
where the time goes:
time: 164 us; the launch traced here: 162 us
  Pallas kernels  119 us (73%)
  matrix products  25.5 us (16%)
  local copies, waits for them, and re-layouts  13.3 us (8%)
  other arithmetic  3.33 us (2%)
    pallas_call x1, Pallas kernels, back_stage(): pl.pallas_call(back_kernel, out_shape=jax.ShapeDtypeStruct((tok, width),...  34.7 us
    pallas_call x1, Pallas kernels, norm_stage(): pl.pallas_call(functools.partial(norm_kernel, count), out_shape=(jax.Shap...  31.8 us
    pallas_call x1, Pallas kernels, attend(): pl.pallas_call(functools.partial(attend_kernel, count), out_shape=(jax.Sh...  27 us
    pallas_call x1, Pallas kernels, grads_stage(): pl.pallas_call(functools.partial(grads_kernel, count), out_shape=(jax.Sha...  25.4 us
    unnamed x54, local copies, waits for them, and re-layouts  13.3 us
    dot_general x2, matrix products, dot_nt(): lax.dot_general(a, b, (((1,), (1,)), ((), ())), preferred_element_type=F32)  13 us
    dot_general x3, matrix products, dot_nn(): return jnp.dot(a, b, preferred_element_type=F32)  12.6 us

commit v1 on v0

--- a/solution.py
+++ b/solution.py
@@ -10,7 +10,7 @@
 
 HEAD_DIM = 128
 OFFSETS = (-2, -1, 1, 2)
-CHUNKS = 2
+CHUNKS = 4
 TILE = 512
 epsilon = 1e-05
 MESH = pl.DeviceIdType.MESH
@@ -102,9 +102,22 @@
 
 
 def attend_kernel(
-    count, q_ref, k_ref, v_ref, out_ref, kwin, vwin, stat_ref, prob, ks, kr, vs, vr
+    count, q_ref, k_ref, v_ref, cot_ref, down_ref,
+    out_ref, kwin, vwin, stat_ref, gm_ref,
+    prob, cot_buf, down_buf, ks, kr, vs, vr, cot_sem, down_sem,
 ):
     blocks = Blocks(count)
+    pieces, depth = down_buf.shape[:2]
+    cot_copy = pltpu.make_async_copy(cot_ref, cot_buf, cot_sem)
+    cot_copy.start()
+    loads = [
+        pltpu.make_async_copy(
+            down_ref.at[pl.ds(i * depth, depth)], down_buf.at[i], down_sem.at[i]
+        )
+        for i in range(pieces)
+    ]
+    for load in loads:
+        load.start()
     barrier = pltpu.get_barrier_semaphore()
     blocks.greet(barrier)
     blocks.greeted(barrier)
@@ -114,6 +127,10 @@
     blocks.clear(vwin)
     rows, width = q_ref.shape
     heads = width // HEAD_DIM
+    cot_copy.wait()
+    for i in range(pieces):
+        loads[i].wait()
+        gm_ref[:, i * depth : (i + 1) * depth] = dot_nt(cot_buf[...], down_buf[i])
     for index in range(4):
         blocks.arrive(k_ref, kwin, ks, kr, index)
     bias = [jnp.where(blocks.there(offset), 0.0, -1e30).astype(F32) for offset in OFFSETS]
@@ -151,8 +168,10 @@
     blocks.left(v_ref, vwin, vs, vr)
 
 
-def attend(count, q, k, v):
+def attend(count, q, k, v, cotangent, down):
     rows, width = q.shape
+    src, model = down.shape
+    pieces = 4
     heads = width // HEAD_DIM
     win = jax.ShapeDtypeStruct((4, rows, width), BF16)
     dma = pltpu.SemaphoreType.DMA((4,))
@@ -163,15 +182,23 @@
             win,
             win,
             jax.ShapeDtypeStruct((2 * heads, rows), F32),
+            jax.ShapeDtypeStruct((rows, src), F32),
         ),
-        in_specs=[pl.BlockSpec(memory_space=VM)] * 3,
-        out_specs=(pl.BlockSpec(memory_space=VM),) * 4,
-        scratch_shapes=[VM((heads, 5, rows, rows), BF16), dma, dma, dma, dma],
+        in_specs=[pl.BlockSpec(memory_space=VM)] * 3 + [pl.BlockSpec(memory_space=pl.ANY)] * 2,
+        out_specs=(pl.BlockSpec(memory_space=VM),) * 5,
+        scratch_shapes=[
+            VM((heads, 5, rows, rows), BF16),
+            VM(cotangent.shape, BF16),
+            VM((pieces, src // pieces, model), BF16),
+            dma, dma, dma, dma,
+            pltpu.SemaphoreType.DMA(()),
+            pltpu.SemaphoreType.DMA((pieces,)),
+        ],
         compiler_params=pltpu.CompilerParams(
-            collective_id=1, has_side_effects=True, vmem_limit_bytes=32 << 20
+            collective_id=1, has_side_effects=True, vmem_limit_bytes=48 << 20
         ),
         name="attend",
-    )(q, k, v)
+    )(q, k, v, cotangent, down)
 
 
 def reduce_first(group, own, part, mine, sbuf1, rbuf1, s1, r1):
@@ -329,14 +356,26 @@
 
 
 def back_kernel(
-    gh_ref, w_ref, cot_ref, gain_ref, unit_ref, sigma_ref,
-    full,
-    mine, sbuf1, rbuf1, sbuf2, rbuf2, cot_buf,
-    s1, r1, s2, r2, ags, agr, cot_sem,
+    gh_ref, up_ref, merged_ref, down_ref, cot_ref, gain_ref, unit_ref, sigma_ref,
+    full, ffn_ref,
+    mine, sbuf1, rbuf1, sbuf2, rbuf2, cot_buf, w_ref, down_buf,
+    s1, r1, s2, r2, ags, agr, cot_sem, up_sem, down_sem,
 ):
     group = Group()
     own, width = unit_ref.shape
     rows = own // CHUNKS
+    tiles = width // TILE
+
+    def up_load(ct):
+        span = pl.ds(pl.multiple_of(ct * TILE, TILE), TILE)
+        return pltpu.make_async_copy(up_ref.at[span], w_ref.at[span], up_sem.at[ct])
+
+    def down_load(ct):
+        span = pl.ds(pl.multiple_of(ct * TILE, TILE), TILE)
+        return pltpu.make_async_copy(down_ref.at[:, span], down_buf.at[ct], down_sem.at[ct])
+
+    for ct in range(tiles):
+        up_load(ct).start()
     fetch = pltpu.make_async_copy(
         cot_ref.at[pl.ds(pl.multiple_of(group.me * own, own), own)], cot_buf, cot_sem
     )
@@ -350,16 +389,26 @@
             [gh_ref[pl.ds(pl.multiple_of(o * own, own), own), :] for o in owners], axis=0
         )
 
-        @pl.loop(0, width // TILE)
+        @pl.loop(0, tiles)
         def _(ct):
+            if dst is sbuf1:
+                up_load(ct).wait()
             cols = pl.ds(pl.multiple_of(ct * TILE, TILE), TILE)
             r = dot_nt(lhs, w_ref[cols, :]).astype(BF16)
             dst[0, :, cols] = r[:own]
             dst[1, :, cols] = r[own:]
 
+    for ct in range(tiles):
+        down_load(ct).start()
     firsts = reduce_first(group, own, part, mine, sbuf1, rbuf1, s1, r1)
     seconds = reduce_second(group, own, mine, rbuf1, sbuf2, rbuf2, s2, r2, firsts)
     fetch.wait()
+
+    @pl.loop(0, tiles)
+    def _(ct):
+        down_load(ct).wait()
+        cols = pl.ds(pl.multiple_of(ct * TILE, TILE), TILE)
+        ffn_ref[:, cols] = dot_nn(merged_ref[...], down_buf[ct]).astype(BF16)
 
     def finish(ch, dst):
         sl = slice(ch * rows, (ch + 1) * rows)
@@ -380,25 +429,27 @@
         copy.wait_send()
 
 
-def back_stage(groups, gh, w, cotangent, gain, unit, sigma):
+def back_stage(groups, gh, up, merged, down, cotangent, gain, unit, sigma):
     tok, width = cotangent.shape
     own = tok // groups
     dma = pltpu.SemaphoreType.DMA
     vm = pl.BlockSpec(memory_space=VM)
+    far = pl.BlockSpec(memory_space=pl.ANY)
+    tiles = width // TILE
     return pl.pallas_call(
         back_kernel,
-        out_shape=jax.ShapeDtypeStruct((tok, width), BF16),
-        in_specs=[vm, vm, pl.BlockSpec(memory_space=pl.ANY), vm, vm, vm],
-        out_specs=vm,
+        out_shape=(jax.ShapeDtypeStruct((tok, width), BF16),) * 2,
+        in_specs=[vm, far, vm, far, far, vm, vm, vm],
+        out_specs=(vm, vm),
         scratch_shapes=reduce_scratch(own, width)
-        + [VM((own, width), BF16)]
+        + [VM((own, width), BF16), VM(up.shape, BF16), VM((tiles, down.shape[0], TILE), BF16)]
         + reduce_sems()
-        + [dma((CHUNKS, 3)), dma((CHUNKS, 3)), dma(())],
+        + [dma((CHUNKS, 3)), dma((CHUNKS, 3)), dma(()), dma((tiles,)), dma((tiles,))],
         compiler_params=pltpu.CompilerParams(
-            collective_id=3, has_side_effects=True, vmem_limit_bytes=40 << 20
+            collective_id=3, has_side_effects=True, vmem_limit_bytes=48 << 20
         ),
         name="back_stage",
-    )(gh, w, cotangent, gain, unit, sigma)
+    )(gh, up, merged, down, cotangent, gain, unit, sigma)
 
 
 def grads_kernel(
@@ -478,18 +529,18 @@
         blocks.arrive(do_ref, dwin, ds_, dr, index)
         blocks.arrive(delta_ref, twin, ts, tr, index)
 
-    @pl.loop(0, heads)
-    def _(h):
-        cols = pl.ds(pl.multiple_of(h * HEAD_DIM, HEAD_DIM), HEAD_DIM)
-        kh, vh = k_ref[:, cols], v_ref[:, cols]
-        gv, gk = gv_ref[:, cols], gk_ref[:, cols]
-        for index in range(4):
-            q_off, g_off = qwin[index, :, cols], dwin[index, :, cols]
-            prob, slope = pair(q_off, kh, vh, g_off, swin.at[index], twin.at[index], h)
-            gv = gv + dot_nn(prob, g_off)
-            gk = gk + dot_nn(slope, q_off)
-        gv_ref[:, cols] = gv
-        gk_ref[:, cols] = gk * SCALE
+        @pl.when(blocks.there(OFFSETS[index]))
+        def _():
+            @pl.loop(0, heads)
+            def _(h):
+                cols = pl.ds(pl.multiple_of(h * HEAD_DIM, HEAD_DIM), HEAD_DIM)
+                kh, vh = k_ref[:, cols], v_ref[:, cols]
+                q_off, g_off = qwin[index, :, cols], dwin[index, :, cols]
+                prob, slope = pair(q_off, kh, vh, g_off, swin.at[index], twin.at[index], h)
+                gv_ref[:, cols] += dot_nn(prob, g_off)
+                gk_ref[:, cols] += dot_nn(slope, q_off)
+
+    gk_ref[...] = gk_ref[...] * SCALE
 
     firsts[1].wait_recv()
     near_rows = ffn_rows(group.me)
@@ -577,7 +628,9 @@
     inverse = 1.0 / counts
     pick = pick.astype(BF16)
 
-    attended, kwin, vwin, stats = attend(count, query_heads, key_heads, value_heads)
+    attended, kwin, vwin, stats, grad_merged = attend(
+        count, query_heads, key_heads, value_heads, cotangent, down_source
+    )
     normed, unit, sigma, qwin, swin = norm_stage(
         count, groups, attended, out_weight, residual, gain, query_heads, stats
     )
@@ -586,13 +639,14 @@
     act_src, slope_src = gelu_slope(hidden_in)
     act_copy, slope_copy = gelu_slope(copies_in)
     merged = ((act_src + dot_nt(act_copy.astype(BF16), pick)) * inverse).astype(BF16)
-    grad_scaled = dot_nt(cotangent, down_source) * inverse
+    grad_scaled = grad_merged * inverse
     grad_copy = dot_nn(grad_scaled.astype(BF16), pick) * slope_copy
     grad_hidden = (
         grad_scaled * slope_src + dot_nt((grad_copy * copy_gain).astype(BF16), pick)
     ).astype(BF16)
-    ffn_part = dot_nn(merged, down_source).astype(BF16)
-    grad_low = back_stage(groups, grad_hidden, up_source, cotangent, gain, unit, sigma)
+    grad_low, ffn_part = back_stage(
+        groups, grad_hidden, up_source, merged, down_source, cotangent, gain, unit, sigma
+    )
     encoded, grad_query, grad_key, grad_value = grads_stage(
         count, grad_low, out_weight, attended, query_heads, key_heads, value_heads,
         kwin, vwin, qwin, stats, swin, ffn_part, unit, gain,

time: 164 us -> 154 us (0.939)
  local copies, waits for them, and re-layouts: 13.3 us -> 7.57 us
  matrix products: 25.5 us -> 20.1 us
  Pallas kernels: 119 us -> 122 us
    unnamed x54 -> x38, local copies, waits for them, and re-layouts: 13.3 us -> 7.57 us
    dot_general x2, matrix products: 13 us -> 9.39 us  [dot_nt(): lax.dot_general(a, b, (((1,), (1,)), ((), ())), preferred_element_type=F32)]
    dot_general x3 -> x2, matrix products: 12.6 us -> 10.7 us  [dot_nn(): return jnp.dot(a, b, preferred_element_type=F32)]
where the time goes in v1:
time: 154 us; the launch traced here: 153 us
  Pallas kernels  122 us (79%)
  matrix products  20.1 us (13%)
  local copies, waits for them, and re-layouts  7.57 us (5%)
  other arithmetic  3.33 us (2%)
    pallas_call x1, Pallas kernels, back_stage(): pl.pallas_call(back_kernel, out_shape=(jax.ShapeDtypeStruct((tok, width),...  36.1 us
    pallas_call x1, Pallas kernels, norm_stage(): pl.pallas_call(functools.partial(norm_kernel, count), out_shape=(jax.Shap...  31.8 us
    pallas_call x1, Pallas kernels, attend(): pl.pallas_call(functools.partial(attend_kernel, count), out_shape=(jax.Sh...  27.1 us
    pallas_call x1, Pallas kernels, grads_stage(): pl.pallas_call(functools.partial(grads_kernel, count), out_shape=(jax.Sha...  26.6 us
    dot_general x2, matrix products, dot_nn(): return jnp.dot(a, b, preferred_element_type=F32)  10.7 us
    dot_general x2, matrix products, dot_nt(): lax.dot_general(a, b, (((1,), (1,)), ((), ())), preferred_element_type=F32)  9.39 us
    unnamed x38, local copies, waits for them, and re-layouts  7.57 us

profile of v1, /device:TPU:10, one launch (start us, length us, event | category | flops | bytes accessed | tf_op | source)
XLA Modules:
  0.0 153.4 jit_solution(6744293359118272556)
XLA Ops:
  0.6 0.7 broadcast_subtract_fusion
  1.3 0.5 convert_reduce_fusion
  1.8 0.0 copy-start.3
  1.8 0.9 copy-done.3
  2.8 0.0 copy-start.7
  2.8 0.9 copy-done.7
  3.7 0.0 copy-start.9
  3.7 0.9 copy-done.9
  4.7 0.0 copy-start
  4.7 0.0 copy-start.4
  4.7 0.0 copy-start.5
  4.7 0.0 copy-start.14
  4.7 27.1 %attend.1 = (bf16[256,512]{1,0:T(8,128)(2,1)S(1)}, bf16[4,256,512]{2,1,0:T(8,128)(2,1)S(1)}, bf16[4,256,512]{2,1,0:T(8,128)(2,1)S(1)}, f32[8,256]{1,0:T(8,128)S(1)}, f32[256,1024]{1,0:T(8,128)S(1)}) custom-call(bf16[256,512]{1,0:T(8,128)(2,1)S(1)} %copy-done.3, bf16[256,512]{1,0:T(8,128)(2,1)S(1)} %copy-done.7, bf16[256,512]{1,0:T(8,128)(2,1)S(1)} %copy-done.9, ...), custom_call_target="tpu_custom_call" | custom-call | tf_op jit(solution)/shard_map/attend/pallas_call | solution.py:178
  31.8 0.0 copy-start.11
  31.9 0.0 copy-start.15
  31.9 0.0 copy-done
  31.9 0.0 copy-done.4
  31.9 0.0 copy-done.5
  31.9 0.0 copy-done.14
  31.9 31.8 %norm_stage.1 = (bf16[256,4096]{1,0:T(8,128)(2,1)S(1)}, f32[64,4096]{1,0:T(8,128)S(1)}, f32[64,128]{1,0:T(8,128)S(1)}, bf16[4,256,512]{2,1,0:T(8,128)(2,1)S(1)}, f32[4,8,256]{2,1,0:T(8,128)S(1)}) custom-call(bf16[256,512]{1,0:T(8,128)(2,1)S(1)} %get-tuple-element.22.att_ref, bf16[512,4096]{1,0:T(8,128)(2,1)S(1)} %copy-done, bf16[256,4096]{1,0:T(8,128)(2,1)S(1)} %copy-done.5, ...), custom_call_target="tpu_custom_call" | custom-call | tf_op jit(solution)/shard_map/norm_stage/pallas_call | solution.py:334
  63.7 0.0 copy-start.6
  63.7 0.0 copy-start.1
  63.7 0.0 copy-start.16
  63.7 7.5 %fusion.57 = f32[256,1024]{1,0:T(8,128)} fusion(bf16[256,4096]{1,0:T(8,128)(2,1)S(1)} %get-tuple-element.24, bf16[4096,1024]{1,0:T(8,128)(2,1)} %up_ref.1), kind=kOutput, calls=%fused_computation.66 | convolution fusion | flops 2147483648 | bytes 11534336 | tf_op jit(solution)/shard_map/dot_general | solution.py:24
  71.2 0.0 copy-done.11
  71.2 0.0 copy-done.15
  71.2 0.0 copy-done.6
  71.2 0.0 copy-done.16
  71.2 3.2 %fusion.10 = f32[256,1024]{1,0:T(8,128)} fusion(s32[1024]{0:T(1024)S(1)} %broadcast_subtract_fusion, f32[1024]{0:T(1024)S(1)} %copy-done.16, f32[256,1024]{1,0:T(8,128)} %fusion.57), kind=kOutput, calls=%fused_computation.16 | convolution fusion | flops 538443776 | bytes 2105344 | tf_op jit(solution)/shard_map/dot_general | solution.py:24
  74.4 6.2 %fusion.15.gh_ref = bf16[256,1024]{1,0:T(8,128)(2,1)} fusion(s32[1024]{0:T(1024)S(1)} %broadcast_subtract_fusion, f32[256,1024]{1,0:T(8,128)} %fusion.57, f32[256,1024]{1,0:T(8,128)} %fusion.10, f32[256,1024]{1,0:T(8,128)} %copy-done.15, f32[1024]{0:T(1024)S(1)} %copy-done.16, f32[1024]{0:T(1024)S(1)} %add_divide_fusion), kind=kOutput, calls=%fused_computation.21 | convolution fusion | flops 1087111168 | bytes 3682304 | tf_op jit(solution)/shard_map/dot_general | solution.py:28
  80.6 0.0 copy-start.13
  80.6 3.2 %fusion.14.merged_ref = bf16[256,1024]{1,0:T(8,128)(2,1)S(1)} fusion(s32[1024]{0:T(1024)S(1)} %broadcast_subtract_fusion, f32[256,1024]{1,0:T(8,128)} %fusion.57, f32[256,1024]{1,0:T(8,128)} %fusion.10, f32[1024]{0:T(1024)S(1)} %add_divide_fusion), kind=kOutput, calls=%fused_computation.20 | convolution fusion | flops 543162368 | bytes 2629632 | tf_op jit(solution)/shard_map/dot_general | solution.py:28
  83.8 0.0 copy-done.1
  83.8 0.0 copy-done.13
  83.8 0.0 copy-start.8
  83.8 0.0 copy-start.10
  83.8 0.0 copy-start.12
  83.9 36.1 %back_stage.1 = (bf16[256,4096]{1,0:T(8,128)(2,1)S(1)}, bf16[256,4096]{1,0:T(8,128)(2,1)}) custom-call(bf16[256,1024]{1,0:T(8,128)(2,1)S(1)} %copy-done.13, bf16[4096,1024]{1,0:T(8,128)(2,1)} %up_ref.1, bf16[256,1024]{1,0:T(8,128)(2,1)S(1)} %fusion.14.merged_ref, bf16[1024,4096]{1,0:T(8,128)(2,1)} %down_ref.3, bf16[256,4096]{1,0:T(8,128)(2,1)} %cot_ref.3, ...), custom_call_target="tpu_custom_call" | custom-call | tf_op jit(solution)/shard_map/back_stage/pallas_call | solution.py:439
  120.0 0.0 copy-start.2
  120.0 1.3 copy-done.2
  121.3 0.0 copy-done.8
  121.3 0.0 copy-done.10
  121.3 0.0 copy-done.12
  121.3 26.6 %grads_stage.1 = (f32[64,4096]{1,0:T(8,128)S(1)}, f32[256,512]{1,0:T(8,128)S(1)}, f32[256,512]{1,0:T(8,128)S(1)}, f32[256,512]{1,0:T(8,128)S(1)}) custom-call(bf16[256,4096]{1,0:T(8,128)(2,1)} %copy-done.2, bf16[512,4096]{1,0:T(8,128)(2,1)} %w_ref.3, bf16[256,512]{1,0:T(8,128)(2,1)S(1)} %copy-done.12, bf16[256,512]{1,0:T(8,128)(2,1)S(1)} %copy-done.4, ...), custom_call_target="tpu_custom_call" | custom-call | tf_op jit(solution)/shard_map/grads_stage/pallas_call | solution.py:575
  147.9 2.1 %dynamic-slice_convert_fusion = f32[256,1024]{1,0:T(8,128)} fusion(bf16[256,4096]{1,0:T(8,128)(2,1)} %copy-done.2, s32[]{:T(128)S(6)} %select_n.3), kind=kLoop, calls=%fused_computation.40 | loop fusion | flops 262144 | bytes 1572868 | tf_op jit(solution)/shard_map/convert_element_type | solution.py:656
  150.0 1.0 copy.20
  151.0 0.8 copy.21
  151.8 0.8 copy.22
  152.6 0.8 copy.23
  (1 shorter events, 0.0 us)
Async XLA Ops:
  1.8 1.0 copy-start.3
  2.8 0.9 copy-start.7
  3.7 0.9 copy-start.9
  4.7 27.2 %copy-start = (bf16[512,4096]{1,0:T(8,128)(2,1)S(1)}, bf16[512,4096]{1,0:T(8,128)(2,1)}, u32[]{:S(2)}) copy-start(bf16[512,4096]{1,0:T(8,128)(2,1)} %w_ref.3) | copy-start | bytes 12582916
  4.7 27.2 %copy-start.4 = (bf16[256,512]{1,0:T(8,128)(2,1)S(1)}, bf16[256,512]{1,0:T(8,128)(2,1)}, u32[]{:S(2)}) copy-start(bf16[256,512]{1,0:T(8,128)(2,1)} %q_ref.5) | copy-start | bytes 786436
  4.7 27.2 %copy-start.5 = (bf16[256,4096]{1,0:T(8,128)(2,1)S(1)}, bf16[256,4096]{1,0:T(8,128)(2,1)}, u32[]{:S(2)}) copy-start(bf16[256,4096]{1,0:T(8,128)(2,1)} %res_ref.1) | copy-start | bytes 6291460
  4.7 27.2 %copy-start.14 = (f32[4096]{0:T(1024)S(1)}, f32[4096]{0:T(1024)}, u32[]{:S(2)}) copy-start(f32[4096]{0:T(1024)} %param.16) | copy-start | bytes 49156
  31.8 39.4 %copy-start.11 = (bf16[256,512]{1,0:T(8,128)(2,1)}, bf16[256,512]{1,0:T(8,128)(2,1)S(1)}, u32[]{:S(2)}) copy-start(bf16[256,512]{1,0:T(8,128)(2,1)S(1)} %get-tuple-element.22.att_ref) | copy-start | bytes 786436
  31.9 39.3 %copy-start.15 = (f32[256,1024]{1,0:T(8,128)}, f32[256,1024]{1,0:T(8,128)S(1)}, u32[]{:S(2)}) copy-start(f32[256,1024]{1,0:T(8,128)S(1)} %get-tuple-element.21) | copy-start | bytes 3145732
  63.7 7.5 %copy-start.6 = (bf16[4,256,512]{2,1,0:T(8,128)(2,1)}, bf16[4,256,512]{2,1,0:T(8,128)(2,1)S(1)}, u32[]{:S(2)}) copy-start(bf16[4,256,512]{2,1,0:T(8,128)(2,1)S(1)} %get-tuple-element.30.qwin) | copy-start | bytes 3145732
  63.7 20.1 %copy-start.1 = (f32[64,4096]{1,0:T(8,128)}, f32[64,4096]{1,0:T(8,128)S(1)}, u32[]{:S(2)}) copy-start(f32[64,4096]{1,0:T(8,128)S(1)} %get-tuple-element.25.unit_ref) | copy-start | bytes 3145732
  63.7 7.5 %copy-start.16 = (f32[1024]{0:T(1024)S(1)}, f32[1024]{0:T(1024)}, u32[]{:S(2)}) copy-start(f32[1024]{0:T(1024)} %param.19) | copy-start | bytes 12292
  80.6 3.2 %copy-start.13 = (bf16[256,1024]{1,0:T(8,128)(2,1)S(1)}, bf16[256,1024]{1,0:T(8,128)(2,1)}, u32[]{:S(2)}) copy-start(bf16[256,1024]{1,0:T(8,128)(2,1)} %fusion.15.gh_ref) | copy-start | bytes 1572868
  83.8 37.5 %copy-start.8 = (bf16[256,512]{1,0:T(8,128)(2,1)S(1)}, bf16[256,512]{1,0:T(8,128)(2,1)}, u32[]{:S(2)}) copy-start(bf16[256,512]{1,0:T(8,128)(2,1)} %k_ref.3) | copy-start | bytes 786436
  83.8 37.5 %copy-start.10 = (bf16[256,512]{1,0:T(8,128)(2,1)S(1)}, bf16[256,512]{1,0:T(8,128)(2,1)}, u32[]{:S(2)}) copy-start(bf16[256,512]{1,0:T(8,128)(2,1)} %v_ref.3) | copy-start | bytes 786436
  83.8 37.5 %copy-start.12 = (bf16[256,512]{1,0:T(8,128)(2,1)S(1)}, bf16[256,512]{1,0:T(8,128)(2,1)}, u32[]{:S(2)}) copy-start(bf16[256,512]{1,0:T(8,128)(2,1)} %copy-done.11) | copy-start | bytes 786436
  120.0 1.3 copy-start.2

commit v2 on v1

--- a/solution.py
+++ b/solution.py
@@ -254,9 +254,10 @@
 
 def norm_kernel(
     count, att_ref, w_ref, res_ref, gain_ref, q_ref, stat_ref,
-    full, unit_ref, sigma_ref, qwin, swin,
-    mine, sbuf1, rbuf1, sbuf2, rbuf2, res_buf,
-    s1, r1, s2, r2, ags, agr, qs, qr, ss, sr, res_sem,
+    up_ref, pick_ref, gm_ref, inv_ref, cg_ref,
+    merged_ref, gh_ref, unit_ref, sigma_ref, qwin, swin,
+    mine, sbuf1, rbuf1, sbuf2, rbuf2, res_buf, full, up_buf,
+    s1, r1, s2, r2, ags, agr, qs, qr, ss, sr, res_sem, up_sem,
 ):
     blocks, group = Blocks(count), Group()
     own, width = unit_ref.shape
@@ -265,6 +266,8 @@
         res_ref.at[pl.ds(pl.multiple_of(group.me * own, own), own)], res_buf, res_sem
     )
     fetch.start()
+    up_load = pltpu.make_async_copy(up_ref, up_buf, up_sem)
+    up_load.start()
     barrier = pltpu.get_barrier_semaphore()
     group.greet(barrier)
     blocks.greet(barrier)
@@ -306,6 +309,24 @@
         dst[...] = (unit * gain_ref[...]).astype(BF16)
 
     tails = spread(group, own, full, finish, seconds, ags, agr)
+    up_load.wait()
+    half = 2 * own
+
+    @pl.loop(0, full.shape[0] // half)
+    def _(b):
+        span = pl.ds(pl.multiple_of(b * half, half), half)
+        hidden = dot_nn(full[span, :], up_buf[...])
+        copies = dot_nn(hidden.astype(BF16), pick_ref[...]) * cg_ref[...]
+        act_src, slope_src = gelu_slope(hidden)
+        act_copy, slope_copy = gelu_slope(copies)
+        summed = act_src + dot_nt(act_copy.astype(BF16), pick_ref[...])
+        merged_ref[span, :] = (summed * inv_ref[...]).astype(BF16)
+        scaled = gm_ref[span, :] * inv_ref[...]
+        grad_copy = dot_nn(scaled.astype(BF16), pick_ref[...]) * slope_copy * cg_ref[...]
+        gh_ref[span, :] = (
+            scaled * slope_src + dot_nt(grad_copy.astype(BF16), pick_ref[...])
+        ).astype(BF16)
+
     for copy in firsts + seconds + tails:
         copy.wait_send()
     for index in range(4):
@@ -326,33 +347,35 @@
     return [dma((2,)), dma((2,)), dma((CHUNKS,)), dma((CHUNKS,))]
 
 
-def norm_stage(count, groups, att, w, residual, gain, q, stats):
+def norm_stage(count, groups, att, w, residual, gain, q, stats, up, pick, gm, inverse, copy_gain):
     tok, width = residual.shape
     own = tok // groups
     dma = pltpu.SemaphoreType.DMA
     vm = pl.BlockSpec(memory_space=VM)
+    far = pl.BlockSpec(memory_space=pl.ANY)
     return pl.pallas_call(
         functools.partial(norm_kernel, count),
         out_shape=(
-            jax.ShapeDtypeStruct((tok, width), BF16),
+            jax.ShapeDtypeStruct(gm.shape, BF16),
+            jax.ShapeDtypeStruct(gm.shape, BF16),
             jax.ShapeDtypeStruct((own, width), F32),
             jax.ShapeDtypeStruct((own, 128), F32),
             jax.ShapeDtypeStruct((4,) + q.shape, BF16),
             jax.ShapeDtypeStruct((4,) + stats.shape, F32),
         ),
-        in_specs=[vm, vm, pl.BlockSpec(memory_space=pl.ANY), vm, vm, vm],
-        out_specs=(vm,) * 5,
+        in_specs=[vm, vm, far, vm, vm, vm, far, vm, vm, vm, vm],
+        out_specs=(vm,) * 6,
         scratch_shapes=reduce_scratch(own, width)
-        + [VM((own, width), BF16)]
+        + [VM((own, width), BF16), VM((tok, width), BF16), VM(up.shape, BF16)]
         + reduce_sems()
         + [dma((CHUNKS, 3)), dma((CHUNKS, 3))]
         + [dma((4,))] * 4
-        + [dma(())],
+        + [dma(())] * 2,
         compiler_params=pltpu.CompilerParams(
-            collective_id=2, has_side_effects=True, vmem_limit_bytes=40 << 20
+            collective_id=2, has_side_effects=True, vmem_limit_bytes=48 << 20
         ),
         name="norm_stage",
-    )(att, w, residual, gain, q, stats)
+    )(att, w, residual, gain, q, stats, up, pick, gm, inverse, copy_gain)
 
 
 def back_kernel(
@@ -595,9 +618,13 @@
     )(low, w, att, q, k, v, kwin, vwin, qwin, stats, swin, ffn, unit, gain)
 
 
-def gelu_slope(inputs):
-    output, pull_back = jax.vjp(jax.nn.gelu, inputs)
-    return (output, pull_back(jnp.ones_like(inputs))[0])
+def gelu_slope(v):
+    rate = math.sqrt(2.0 / math.pi)
+    square = v * v
+    bend = jnp.tanh(rate * v * (1.0 + 0.044715 * square))
+    level = 0.5 * (1.0 + bend)
+    slope = level + (0.5 * rate) * v * (1.0 - bend * bend) * (1.0 + 0.134145 * square)
+    return v * level, slope
 
 
 def shards(
@@ -631,19 +658,10 @@
     attended, kwin, vwin, stats, grad_merged = attend(
         count, query_heads, key_heads, value_heads, cotangent, down_source
     )
-    normed, unit, sigma, qwin, swin = norm_stage(
-        count, groups, attended, out_weight, residual, gain, query_heads, stats
-    )
-    hidden_in = dot_nn(normed, up_source)
-    copies_in = dot_nn(hidden_in.astype(BF16), pick) * copy_gain
-    act_src, slope_src = gelu_slope(hidden_in)
-    act_copy, slope_copy = gelu_slope(copies_in)
-    merged = ((act_src + dot_nt(act_copy.astype(BF16), pick)) * inverse).astype(BF16)
-    grad_scaled = grad_merged * inverse
-    grad_copy = dot_nn(grad_scaled.astype(BF16), pick) * slope_copy
-    grad_hidden = (
-        grad_scaled * slope_src + dot_nt((grad_copy * copy_gain).astype(BF16), pick)
-    ).astype(BF16)
+    merged, grad_hidden, unit, sigma, qwin, swin = norm_stage(
+        count, groups, attended, out_weight, residual, gain, query_heads, stats,
+        up_source, pick, grad_merged, inverse[None, :], copy_gain[None, :],
+    )
     grad_low, ffn_part = back_stage(
         groups, grad_hidden, up_source, merged, down_source, cotangent, gain, unit, sigma
     )

time: 154 us -> 145 us (0.942)
  matrix products: 20.1 us -> 0 us
  Pallas kernels: 122 us -> 130 us
  other arithmetic: 3.33 us -> 5.55 us
    dot_general x4 -> x0, matrix products: 20.1 us -> none  [the longest x2 10.7 us: dot_nn(): return jnp.dot(a, b, preferred_element_type=F32)]
    pallas_call x1, Pallas kernels: 31.8 us -> 40.3 us  [norm_stage(): pl.pallas_call(functools.partial(norm_kernel, count), out_shape=(jax.Shap...]
    convert_element_type x0 -> x1, other arithmetic: none -> 2.22 us  [shards(): pick = pick.astype(BF16)]
    unnamed x38 -> x26, local copies, waits for them, and re-layouts: 7.57 us -> 8.49 us
where the time goes in v2:
time: 145 us
  Pallas kernels  130 us (90%)
  local copies, waits for them, and re-layouts  8.49 us (6%)
  other arithmetic  5.55 us (4%)
    pallas_call x1, Pallas kernels, norm_stage(): pl.pallas_call(functools.partial(norm_kernel, count), out_shape=(jax.Shap...  40.3 us
    pallas_call x1, Pallas kernels, back_stage(): pl.pallas_call(back_kernel, out_shape=(jax.ShapeDtypeStruct((tok, width),...  36.4 us
    pallas_call x1, Pallas kernels, attend(): pl.pallas_call(functools.partial(attend_kernel, count), out_shape=(jax.Sh...  27.1 us
    pallas_call x1, Pallas kernels, grads_stage(): pl.pallas_call(functools.partial(grads_kernel, count), out_shape=(jax.Sha...  26.3 us
    unnamed x26, local copies, waits for them, and re-layouts  8.49 us

profile of v2, /device:TPU:10, one launch (start us, length us, event | category | flops | bytes accessed | tf_op | source)
XLA Modules:
  0.0 144.9 jit_solution(17798942214914166388)
XLA Ops:
  0.6 0.7 broadcast_subtract_fusion
  1.3 0.5 convert_reduce_fusion
  1.8 2.2 %fusion.pick_ref = bf16[1024,1024]{1,0:T(8,128)(2,1)} fusion(s32[1024]{0:T(1024)S(1)} %broadcast_subtract_fusion), kind=kLoop, calls=%fused_computation.2 | loop fusion | flops 2097152 | bytes 2101248 | tf_op jit(solution)/shard_map/convert_element_type | solution.py:656
  4.1 0.0 copy-start.2
  4.1 0.9 copy-done.2
  5.0 0.0 copy-start.5
  5.0 0.9 copy-done.5
  6.0 0.0 copy-start.7
  6.0 0.9 copy-done.7
  6.9 0.0 copy-start.9
  6.9 0.0 copy-start.10
  6.9 27.1 %attend.1 = (bf16[256,512]{1,0:T(8,128)(2,1)S(1)}, bf16[4,256,512]{2,1,0:T(8,128)(2,1)S(1)}, bf16[4,256,512]{2,1,0:T(8,128)(2,1)S(1)}, f32[8,256]{1,0:T(8,128)S(1)}, f32[256,1024]{1,0:T(8,128)S(1)}) custom-call(bf16[256,512]{1,0:T(8,128)(2,1)S(1)} %copy-done.2, bf16[256,512]{1,0:T(8,128)(2,1)S(1)} %copy-done.5, bf16[256,512]{1,0:T(8,128)(2,1)S(1)} %copy-done.7, ...), custom_call_target="tpu_custom_call" | custom-call | tf_op jit(solution)/shard_map/attend/pallas_call | solution.py:178
  34.0 0.0 copy-done.9
  34.0 0.0 copy-done.10
  34.0 40.3 %norm_stage.1 = (bf16[256,1024]{1,0:T(8,128)(2,1)S(1)}, bf16[256,1024]{1,0:T(8,128)(2,1)S(1)}, f32[64,4096]{1,0:T(8,128)S(1)}, f32[64,128]{1,0:T(8,128)S(1)}, bf...) custom-call(bf16[256,512]{1,0:T(8,128)(2,1)S(1)} %get-tuple-element.22.att_ref, bf16[512,4096]{1,0:T(8,128)(2,1)} %w_ref.3, ...), custom_call_target="tpu_custom_call" | custom-call | tf_op jit(solution)/shard_map/norm_stage/pallas_call | solution.py:356
  74.3 0.0 copy-start.4
  74.3 1.0 copy-done.4
  75.3 0.0 copy-start
  75.3 0.0 copy-start.3
  75.3 0.0 copy-start.6
  75.3 0.0 copy-start.8
  75.3 36.4 %back_stage.1 = (bf16[256,4096]{1,0:T(8,128)(2,1)S(1)}, bf16[256,4096]{1,0:T(8,128)(2,1)}) custom-call(bf16[256,1024]{1,0:T(8,128)(2,1)S(1)} %get-tuple-element.25.gh_ref, bf16[4096,1024]{1,0:T(8,128)(2,1)} %up_ref.3, bf16[256,1024]{1,0:T(8,128)(2,1)S(1)} %get-tuple-element.26.merged_ref, bf16[1024,4096]{1,0:T(8,128)(2,1)} %down_ref.3, ...), custom_call_target="tpu_custom_call" | custom-call | tf_op jit(solution)/shard_map/back_stage/pallas_call | solution.py:462
  111.7 0.0 copy-done
  111.8 0.0 copy-start.1
  111.8 1.3 copy-done.1
  113.1 0.0 copy-done.3
  113.1 0.0 copy-done.6
  113.1 0.0 copy-done.8
  113.1 26.3 %grads_stage.1 = (f32[64,4096]{1,0:T(8,128)S(1)}, f32[256,512]{1,0:T(8,128)S(1)}, f32[256,512]{1,0:T(8,128)S(1)}, f32[256,512]{1,0:T(8,128)S(1)}) custom-call(bf16[256,4096]{1,0:T(8,128)(2,1)} %copy-done.1, bf16[512,4096]{1,0:T(8,128)(2,1)} %w_ref.3, bf16[256,512]{1,0:T(8,128)(2,1)S(1)} %get-tuple-element.22.att_ref, bf16[256,512]{1,0:T(8,128)(2,1)S(1)} %copy-done.3, ...), custom_call_target="tpu_custom_call" | custom-call | tf_op jit(solution)/shard_map/grads_stage/pallas_call | solution.py:598
  139.4 2.1 %dynamic-slice_convert_fusion = f32[256,1024]{1,0:T(8,128)} fusion(bf16[256,4096]{1,0:T(8,128)(2,1)} %copy-done.1, s32[]{:T(128)S(6)} %select_n.3), kind=kLoop, calls=%fused_computation.3 | loop fusion | flops 262144 | bytes 1572868 | tf_op jit(solution)/shard_map/convert_element_type | solution.py:674
  141.5 1.0 copy.20
  142.5 0.8 copy.21
  143.3 0.8 copy.22
  144.1 0.8 copy.23
  (1 shorter events, 0.0 us)
Async XLA Ops:
  4.1 0.9 copy-start.2
  5.0 0.9 copy-start.5
  6.0 0.9 copy-start.7
  6.9 27.1 %copy-start.9 = (f32[4096]{0:T(1024)S(1)}, f32[4096]{0:T(1024)}, u32[]{:S(2)}) copy-start(f32[4096]{0:T(1024)} %param.16) | copy-start | bytes 49156
  6.9 27.1 %copy-start.10 = (f32[1024]{0:T(1024)S(1)}, f32[1024]{0:T(1024)}, u32[]{:S(2)}) copy-start(f32[1024]{0:T(1024)} %param.19) | copy-start | bytes 12292
  74.3 1.0 copy-start.4
  75.3 36.5 %copy-start = (f32[64,4096]{1,0:T(8,128)}, f32[64,4096]{1,0:T(8,128)S(1)}, u32[]{:S(2)}) copy-start(f32[64,4096]{1,0:T(8,128)S(1)} %get-tuple-element.27.unit_ref) | copy-start | bytes 3145732
  75.3 37.8 %copy-start.3 = (bf16[256,512]{1,0:T(8,128)(2,1)S(1)}, bf16[256,512]{1,0:T(8,128)(2,1)}, u32[]{:S(2)}) copy-start(bf16[256,512]{1,0:T(8,128)(2,1)} %q_ref.5) | copy-start | bytes 786436
  75.3 37.8 %copy-start.6 = (bf16[256,512]{1,0:T(8,128)(2,1)S(1)}, bf16[256,512]{1,0:T(8,128)(2,1)}, u32[]{:S(2)}) copy-start(bf16[256,512]{1,0:T(8,128)(2,1)} %k_ref.3) | copy-start | bytes 786436
  75.3 37.8 %copy-start.8 = (bf16[256,512]{1,0:T(8,128)(2,1)S(1)}, bf16[256,512]{1,0:T(8,128)(2,1)}, u32[]{:S(2)}) copy-start(bf16[256,512]{1,0:T(8,128)(2,1)} %v_ref.3) | copy-start | bytes 786436
  111.8 1.3 copy-start.1
